TPU v7x, 128 devices: a whole 4x4x4 slice. The times are simulated.
128 devices in a mesh: ta: 4 (over x), ha: 4 (over y_hi, core), wa: 8 (over z, y_lo).
Axes of the slice: x: 4, y: 4 (y_hi: 2, y_lo: 2; y = y_hi * 2 + y_lo), z: 4, core: 2. Of those that a mesh axis runs over, the one named last changes fastest.
Arguments:
- tokens: bfloat16 [12, 32, 64, 1536], P('ta', 'ha', 'wa'), may hold values from -6 to 6
- modulation: float32 [3, 1536], replicated, may hold values from -4 to 4
- w_query: bfloat16 [1536, 1536], replicated
- w_key: bfloat16 [1536, 1536], replicated
- w_value: bfloat16 [1536, 1536], replicated, may hold values from -0.15625 to 0.15625
- w_out: bfloat16 [1536, 1536], replicated, may hold values from -0.15625 to 0.15625
- norm_q: float32 [1536], replicated, may hold values from 0.8 to 1.6
- norm_k: float32 [1536], replicated, may hold values from 0.8 to 1.6
Outputs:
- branch: bfloat16 [12, 32, 64, 1536], P('ta', 'ha', 'wa')
All inputs are finite; a program needn't handle non-finite values.
Results may differ from a plain program's by a relative error of at most 0.0051.
Values may be sent and summed in bfloat16 or wider, within the bound.
A program may use at most 192 MiB of HBM per device.

v0:
```python
import jax
import jax.numpy as jnp
from jax import lax
from jax.sharding import PartitionSpec as P

HEADS = 12
HEAD_DIM = 128
D = 1536
TT = 3
TH = 8
TW = 8
CT = 3
CH = 8
CW = 8


def with_halo(value, sides, width):
    for axis, dim in sides:
        devices, length = (lax.axis_size(axis), value.shape[dim])
        up = [(i, (i + 1) % devices) for i in range(devices - 1)]
        down = [(j, i) for i, j in up]
        last = lax.slice_in_dim(value, length - width, length, axis=dim)
        first = lax.slice_in_dim(value, 0, width, axis=dim)
        before = lax.ppermute(last, axis, up)
        after = lax.ppermute(first, axis, down)
        value = jnp.concatenate([before, value, after], axis=dim)
    return value


def modulate(tokens, modulation):
    values = tokens.astype(jnp.float32)
    center = values - jnp.mean(values, axis=-1, keepdims=True)
    spread = jnp.mean(center * center, axis=-1, keepdims=True)
    return (center * lax.rsqrt(spread + 1e-06) * (1.0 + modulation[1]) + modulation[0]).astype(
        jnp.bfloat16
    )


def rms_gain(values, gain):
    return values * lax.rsqrt(jnp.mean(values * values, axis=-1, keepdims=True) + 1e-06) * gain


def rotate_pairs(values, frame_pos, row_pos, column_pos):
    half = HEAD_DIM // 2
    sixth = HEAD_DIM // 6
    first = half - 2 * sixth
    freq_first = 10000.0 ** (-jnp.arange(first, dtype=jnp.float32) / first)
    freq_rest = 10000.0 ** (-jnp.arange(sixth, dtype=jnp.float32) / sixth)
    shape = values.shape[:3]
    angle_frame = frame_pos[:, None] * freq_first
    angle_row = row_pos[:, None] * freq_rest
    angle_column = column_pos[:, None] * freq_rest
    angles = jnp.concatenate(
        [
            jnp.broadcast_to(angle_frame[:, None, None, :], shape + (first,)),
            jnp.broadcast_to(angle_row[None, :, None, :], shape + (sixth,)),
            jnp.broadcast_to(angle_column[None, None, :, :], shape + (sixth,)),
        ],
        axis=-1,
    )
    cosine = jnp.cos(angles)[:, :, :, None, :]
    sine = jnp.sin(angles)[:, :, :, None, :]
    pairs = values.reshape(shape + (HEADS, half, 2))
    even_part = pairs[..., 0]
    odd_part = pairs[..., 1]
    rotated = jnp.stack(
        [even_part * cosine - odd_part * sine, even_part * sine + odd_part * cosine], axis=-1
    )
    return rotated.reshape(values.shape)


def tile_rows(query, key_pad, value_pad, anchor, extent):
    tile_frames = CT // TT
    tile_rows_n = CH // TH
    tile_columns = CW // TW
    tile_size = TT * TH * TW
    window = 27 * tile_size

    def one_row(index):
        frame_tile = index // tile_rows_n
        row_tile = index % tile_rows_n
        query_row = query
        query_row = query_row.reshape(TT, TH, tile_columns, TW, HEADS, HEAD_DIM).transpose(
            4, 2, 0, 1, 3, 5
        )
        query_row = query_row.reshape(HEADS, tile_columns, tile_size, HEAD_DIM)
        key_tiles = jnp.stack([key_pad])
        value_tiles = jnp.stack([value_pad])
        key_tiles = key_tiles.reshape(tile_columns, window, HEADS, HEAD_DIM).transpose(2, 0, 1, 3)
        value_tiles = value_tiles.reshape(tile_columns, window, HEADS, HEAD_DIM).transpose(
            2, 0, 1, 3
        )
        frames_at = anchor[0] + frame_tile * TT - TT + jnp.arange(3 * TT, dtype=jnp.int32)
        rows_at = anchor[1] + row_tile * TH - TH + jnp.arange(3 * TH, dtype=jnp.int32)
        columns_at = (
            anchor[2]
            + jnp.arange(tile_columns, dtype=jnp.int32)[:, None] * TW
            - TW
            + jnp.arange(3 * TW, dtype=jnp.int32)[None, :]
        )
        frame_ok = (frames_at >= 0) & (frames_at < extent[0])
        row_ok = (rows_at >= 0) & (rows_at < extent[1])
        column_ok = (columns_at >= 0) & (columns_at < extent[2])
        valid = (
            frame_ok[None, :, None, None]
            & row_ok[None, None, :, None]
            & column_ok[:, None, None, :]
        )
        valid = valid.reshape(tile_columns, window)

        def one_head(operands):
            head_query, head_key, head_value = operands
            scores = jnp.einsum(
                "cqd,ckd->cqk", head_query, head_key, preferred_element_type=jnp.float32
            ) * HEAD_DIM ** (-0.5)
            scores = jnp.where(valid[:, None, :], scores, -1e30)
            peak = jnp.max(scores, axis=-1, keepdims=True)
            expo = jnp.exp(scores - peak)
            weights = (expo / jnp.sum(expo, axis=-1, keepdims=True)).astype(jnp.bfloat16)
            return jnp.einsum(
                "cqk,ckd->cqd", weights, head_value, preferred_element_type=jnp.float32
            ).astype(jnp.bfloat16)

        attended = lax.map(one_head, (query_row, key_tiles, value_tiles))
        attended = attended.reshape(HEADS, tile_columns, TT, TH, TW, HEAD_DIM).transpose(
            2, 3, 1, 4, 0, 5
        )
        return attended.reshape(TT, TH, CW, D)

    result = lax.map(one_row, jnp.arange(tile_frames * tile_rows_n, dtype=jnp.int32))
    result = result.reshape(tile_frames, tile_rows_n, TT, TH, CW, D).transpose(0, 2, 1, 3, 4, 5)
    return result.reshape(CT, CH, CW, D)


def body(tokens, modulation, w_query, w_key, w_value, w_out, norm_q, norm_k):
    anchor = (lax.axis_index("ta") * CT, lax.axis_index("ha") * CH, lax.axis_index("wa") * CW)
    extent = (lax.axis_size("ta") * CT, lax.axis_size("ha") * CH, lax.axis_size("wa") * CW)
    frame_pos = (anchor[0] + jnp.arange(CT, dtype=jnp.int32)).astype(jnp.float32)
    row_pos = (anchor[1] + jnp.arange(CH, dtype=jnp.int32)).astype(jnp.float32)
    column_pos = (anchor[2] + jnp.arange(CW, dtype=jnp.int32)).astype(jnp.float32)
    grid = (CT, CH, CW, D)
    normed = modulate(tokens, modulation)
    flat = normed.reshape(-1, D)
    key = rms_gain(jnp.dot(flat, w_key, preferred_element_type=jnp.float32), norm_k).reshape(grid)
    key = rotate_pairs(key, frame_pos, row_pos, column_pos).astype(jnp.bfloat16)
    value = (
        jnp.dot(flat, w_value, preferred_element_type=jnp.float32)
        .astype(jnp.bfloat16)
        .reshape(grid)
    )
    key_value = jnp.stack([key, value])
    framed = with_halo(key_value, (("ta", 1),), TT)
    padded = with_halo(framed, (("ha", 2), ("wa", 3)), TW)
    query = rms_gain(jnp.dot(flat, w_query, preferred_element_type=jnp.float32), norm_q).reshape(
        grid
    )
    query = rotate_pairs(query, frame_pos, row_pos, column_pos).astype(jnp.bfloat16)
    attended = tile_rows(query, padded[0], padded[1], anchor, extent)
    branch = (
        jnp.dot(attended.reshape(-1, D), w_out, preferred_element_type=jnp.float32) * modulation[2]
    )
    return branch.astype(jnp.bfloat16).reshape(grid)


def solution(mesh):
    in_specs = (P("ta", "ha", "wa", None), P(), P(), P(), P(), P(), P(), P())
    out_specs = P("ta", "ha", "wa", None)
    return jax.shard_map(body, mesh=mesh, in_specs=in_specs, out_specs=out_specs, check_vma=False)
```

profile of v0, /device:TPU:90, one launch (start us, length us, event | category | flops | bytes accessed | tf_op | source)
XLA Modules:
  0.0 832.9 jit_solution(16748141721264547690)
XLA Ops:
  5.6 3.5 multiply_reduce_fusion
  9.8 9.5 %reshape_reshape.7 = f32[3,8,8,12,64,2]{2,1,0,5,4,3:T(8,128)} reshape(f32[192,1536]{0,1:T(8,128)S(1)} %copy.38) | data formatting | bytes 2359296 | tf_op jit(solution)/shard_map/reshape;reshape | solution.py:63
  22.4 3.5 multiply_reduce_fusion.1
  26.6 9.6 %reshape_reshape.6 = f32[3,8,8,12,64,2]{2,1,0,5,4,3:T(8,128)} reshape(f32[192,1536]{0,1:T(8,128)S(1)} %copy.31) | data formatting | bytes 2359296 | tf_op jit(solution)/shard_map/reshape;reshape | solution.py:63
  36.2 3.5 convolution_convert_fusion
  39.8 20.9 %multiply_subtract_fusion = (bf16[3,8,8,12,64,1]{2,1,0,5,4,3:T(8,128)(2,1)}, bf16[3,8,8,12,64,1]{2,1,0,5,4,3:T(8,128)(2,1)}, bf16[3,8,8,12,64,1]{2,1,0,5,4,3:T(8,128)(2,1)}, bf16[3,8,8,12,64,1]{2,1,0,5,4,3:T(8,128)(2,1)}) fusion(f32[3,8,8,12,64,2]{2,1,0,5,4,3:T(8,128)} %reshape_reshape.7, f32[3,8,8,64]{2,1,0,3:T(8,128)S(1)} %copy-done.2, ...), kind=kLoop, calls=%fused_computation.22 | loop fusion | flops 2359296 | bytes 3637248 | tf_op jit(solution)/shard_map/sub | solution.py:67
  60.6 4.5 copy.40
  65.1 4.5 copy.39
  69.8 7.3 copy.41
  77.1 9.3 %copy.42 = bf16[1,3,8,8,1536]{4,3,2,1,0:T(8,128)(2,1)S(1)} copy(bf16[1,3,8,8,1536]{3,2,4,1,0:T(8,128)(2,1)} %bitcast.67) | data formatting | bytes 1179648 | tf_op jit(solution)/shard_map/convert_element_type | solution.py:145
  89.0 3.4 collective-permute-start
  92.4 23.7 %collective-permute-done.1 = bf16[2,3,8,8,1536]{4,3,2,1,0:T(8,128)(2,1)S(1)} collective-permute-done((bf16[2,3,8,8,1536]{4,3,2,1,0:T(8,128)(2,1)S(1)}, bf16[2,3,8,8,1536]{4,3,2,1,0:T(8,128)(2,1)S(1)}, u32[]{:S(2)}, u32[]{:S(2)}) %collective-permute-start.1) | collective-permute-done | bytes 1179680 | tf_op jit(solution)/shard_map/ppermute | solution.py:25
  120.8 2.6 collective-permute-start.2
  123.4 57.5 %collective-permute-done.3 = bf16[2,9,8,8,1536]{4,3,2,1,0:T(8,128)(2,1)S(1)} collective-permute-done((bf16[2,9,8,8,1536]{4,3,2,1,0:T(8,128)(2,1)S(1)}, bf16[2,9,8,8,1536]{4,3,2,1,0:T(8,128)(2,1)S(1)}, u32[]{:S(2)}, u32[]{:S(2)}) %collective-permute-start.3) | collective-permute-done | bytes 3538976 | tf_op jit(solution)/shard_map/ppermute | solution.py:25
  180.9 9.2 %collective-permute-done.2 = bf16[2,9,8,8,1536]{4,3,2,1,0:T(8,128)(2,1)S(1)} collective-permute-done((bf16[2,9,8,8,1536]{4,3,2,1,0:T(8,128)(2,1)S(1)}, bf16[2,9,8,8,1536]{4,3,2,1,0:T(8,128)(2,1)S(1)}, u32[]{:S(2)}, u32[]{:S(2)}) %collective-permute-start.2) | collective-permute-done | bytes 3538976 | tf_op jit(solution)/shard_map/ppermute | solution.py:24
  190.1 5.6 pad_maximum_fusion.1
  195.8 2.9 collective-permute-start.5
  198.7 3.9 collective-permute-start.4
  202.6 5.2 copy.35
  207.8 5.2 copy.34
  215.5 7.8 copy.36
  223.2 7.3 copy.37
  230.6 199.5 %collective-permute-done.5 = bf16[2,9,24,8,1536]{4,3,2,1,0:T(8,128)(2,1)} collective-permute-done((bf16[2,9,24,8,1536]{4,3,2,1,0:T(8,128)(2,1)}, bf16[2,9,24,8,1536]{4,3,2,1,0:T(8,128)(2,1)}, u32[]{:S(2)}, u32[]{:S(2)}) %collective-permute-start.5) | collective-permute-done | bytes 10616864 | tf_op jit(solution)/shard_map/ppermute | solution.py:25
  430.0 185.9 %collective-permute-done.4 = bf16[2,9,24,8,1536]{4,3,2,1,0:T(8,128)(2,1)} collective-permute-done((bf16[2,9,24,8,1536]{4,3,2,1,0:T(8,128)(2,1)}, bf16[2,9,24,8,1536]{4,3,2,1,0:T(8,128)(2,1)}, u32[]{:S(2)}, u32[]{:S(2)}) %collective-permute-start.4) | collective-permute-done | bytes 10616864 | tf_op jit(solution)/shard_map/ppermute | solution.py:24
  615.9 33.2 %pad_maximum_fusion = bf16[2,9,24,24,1536]{4,3,2,1,0:T(8,128)(2,1)} fusion(bf16[2,9,24,8,1536]{4,3,2,1,0:T(8,128)(2,1)} %collective-permute-done.5, bf16[2,9,8,8,1536]{4,3,2,1,0:T(8,128)(2,1)} %copy-done, bf16[2,3,8,8,1536]{4,3,2,1,0:T(8,128)(2,1)S(1)} %collective-permute-done.1, bf16[1,3,8,8,1536]{4,3,2,1,0:T(8,128)(2,1)S(1)} %bitcast.72, ...), kind=kLoop, calls=%fused_computation.19 | loop fusion | flops 254803968 | bytes 63700992 | tf_op jit(solution)/shard_map/concatenate | solution.py:26
  649.1 22.0 %fusion.32 = (bf16[1,9,24,24,1536]{4,3,2,1,0:T(8,128)(2,1)}, bf16[1,9,24,24,1536]{4,3,2,1,0:T(8,128)(2,1)}) fusion(bf16[2,9,24,24,1536]{4,3,2,1,0:T(8,128)(2,1)} %pad_maximum_fusion), kind=kLoop, calls=%fused_computation.67 | loop fusion | bytes 63700992 | tf_op jit(solution)/shard_map/slice | solution.py:158
  671.1 29.0 %stack_squeeze.8 = bf16[1,5184,12,128]{3,2,1,0:T(8,128)(2,1)} reshape(bf16[1,9,24,24,1536]{4,3,2,1,0:T(8,128)(2,1)} %get-tuple-element.121) | data formatting | bytes 31850496 | tf_op jit(solution)/shard_map/while/body/eval_jaxpr/reshape;while/body/eval_jaxpr/stack;squeeze | solution.py:89
  700.1 16.9 %copy.44 = bf16[12,1,5184,128]{3,2,1,0:T(8,128)(2,1)} copy(bf16[12,1,5184,128]{3,0,2,1:T(8,128)(2,1)} %bitcast.65) | data formatting | bytes 31850496
  717.0 29.0 %stack_squeeze.9 = bf16[1,5184,12,128]{3,2,1,0:T(8,128)(2,1)} reshape(bf16[1,9,24,24,1536]{4,3,2,1,0:T(8,128)(2,1)} %get-tuple-element.120) | data formatting | bytes 31850496 | tf_op jit(solution)/shard_map/while/body/eval_jaxpr/reshape;while/body/eval_jaxpr/stack;squeeze | solution.py:90
  746.0 16.9 %copy.45 = bf16[12,1,5184,128]{3,2,1,0:T(8,128)(2,1)} copy(bf16[12,1,5184,128]{3,0,2,1:T(8,128)(2,1)} %bitcast.66) | data formatting | bytes 31850496
  762.9 65.7 %while.18 = (s32[]{:T(128)}, bf16[12,1,192,128]{3,2,1,0:T(8,128)(2,1)S(1)}, bf16[12,1,192,128]{3,2,1,0:T(8,128)(2,1)}, bf16[12,1,5184,128]{3,2,1,0:T(8,128)(2,1)...) while((s32[]{:T(128)}, ...), condition=%wide.region_7.8_spmd.clone, body=%wide.region_4.7_spmd.clone.sunk | while | flops 517599936 | bytes 14773069 | solution.py:124
  828.7 4.3 fusion.22
  (113 shorter events, 85.3 us)
Async XLA Ops:
  0.0 9.2 %copy-start.5 = (f32[1536]{0:T(1024)S(1)}, f32[1536]{0:T(1024)}, u32[]{:S(2)}) copy-start(f32[1536]{0:T(1024)} %param.17) | copy-start | bytes 18436
  19.4 6.6 copy-start.6
  36.2 3.6 copy-start.2
  36.2 3.6 copy-start.3
  86.5 29.6 %collective-permute-start.1 = (bf16[2,3,8,8,1536]{4,3,2,1,0:T(8,128)(2,1)S(1)}, bf16[2,3,8,8,1536]{4,3,2,1,0:T(8,128)(2,1)S(1)}, u32[]{:S(2)}, u32[]{:S(2)}) collective-permute-start(bf16[2,3,8,8,1536]{4,3,2,1,0:T(8,128)(2,1)S(1)} %pad_maximum_fusion.5), channel_id=1, source_target_pairs={{32,0},{64,32},{96,64},{33,1},{65,33},{97,65},{34,2},{66,34},{98,6... | collective-permute-start | bytes 3538952 | tf_op jit(solution)/shard_map/ppermute | solution.py:25
  89.0 29.3 %collective-permute-start = (bf16[2,3,8,8,1536]{4,3,2,1,0:T(8,128)(2,1)S(1)}, bf16[2,3,8,8,1536]{4,3,2,1,0:T(8,128)(2,1)S(1)}, u32[]{:S(2)}, u32[]{:S(2)}) collective-permute-start(bf16[2,3,8,8,1536]{4,3,2,1,0:T(8,128)(2,1)S(1)} %pad_maximum_fusion.5), channel_id=1, source_target_pairs={{0,32},{32,64},{64,96},{1,33},{33,65},{65,97},{2,34},{34,66},{66,9... | collective-permute-start | bytes 3538952 | tf_op jit(solution)/shard_map/ppermute | solution.py:24
  118.7 62.2 %collective-permute-start.3 = (bf16[2,9,8,8,1536]{4,3,2,1,0:T(8,128)(2,1)S(1)}, bf16[2,9,8,8,1536]{4,3,2,1,0:T(8,128)(2,1)S(1)}, u32[]{:S(2)}, u32[]{:S(2)}) collective-permute-start(bf16[2,9,8,8,1536]{4,3,2,1,0:T(8,128)(2,1)S(1)} %pad_maximum_fusion.2), channel_id=1, source_target_pairs={{8,0},{16,8},{24,16},{9,1},{17,9},{25,17},{10,2},{18,10},{26,18},{... | collective-permute-start | bytes 10616840 | tf_op jit(solution)/shard_map/ppermute | solution.py:25
  120.8 69.3 %collective-permute-start.2 = (bf16[2,9,8,8,1536]{4,3,2,1,0:T(8,128)(2,1)S(1)}, bf16[2,9,8,8,1536]{4,3,2,1,0:T(8,128)(2,1)S(1)}, u32[]{:S(2)}, u32[]{:S(2)}) collective-permute-start(bf16[2,9,8,8,1536]{4,3,2,1,0:T(8,128)(2,1)S(1)} %pad_maximum_fusion.2), channel_id=1, source_target_pairs={{0,8},{8,16},{16,24},{1,9},{9,17},{17,25},{2,10},{10,18},{18,26},{... | collective-permute-start | bytes 10616840 | tf_op jit(solution)/shard_map/ppermute | solution.py:24
  180.9 14.9 %copy-start = (bf16[2,9,8,8,1536]{4,3,2,1,0:T(8,128)(2,1)}, bf16[2,9,8,8,1536]{4,3,2,1,0:T(8,128)(2,1)S(1)}, u32[]{:S(2)}) copy-start(bf16[2,9,8,8,1536]{4,3,2,1,0:T(8,128)(2,1)S(1)} %collective-permute-done.3) | copy-start | bytes 10616836
  190.1 5.7 copy-start.1
  195.8 234.2 %collective-permute-start.5 = (bf16[2,9,24,8,1536]{4,3,2,1,0:T(8,128)(2,1)}, bf16[2,9,24,8,1536]{4,3,2,1,0:T(8,128)(2,1)}, u32[]{:S(2)}, u32[]{:S(2)}) collective-permute-start(bf16[2,9,24,8,1536]{4,3,2,1,0:T(8,128)(2,1)} %pad_maximum_fusion.1), channel_id=1, source_target_pairs={{1,0},{2,1},{3,2},{4,3},{5,4},{6,5},{7,6},{9,8},{10,9},{11,10},{12... | collective-permute-start | bytes 31850504 | tf_op jit(solution)/shard_map/ppermute | solution.py:25
  198.7 417.3 %collective-permute-start.4 = (bf16[2,9,24,8,1536]{4,3,2,1,0:T(8,128)(2,1)}, bf16[2,9,24,8,1536]{4,3,2,1,0:T(8,128)(2,1)}, u32[]{:S(2)}, u32[]{:S(2)}) collective-permute-start(bf16[2,9,24,8,1536]{4,3,2,1,0:T(8,128)(2,1)} %pad_maximum_fusion.1), channel_id=1, source_target_pairs={{0,1},{1,2},{2,3},{3,4},{4,5},{5,6},{6,7},{8,9},{9,10},{10,11},{11... | collective-permute-start | bytes 31850504 | tf_op jit(solution)/shard_map/ppermute | solution.py:24
  746.0 16.9 %copy-start.4 = (bf16[12,1,192,128]{3,2,1,0:T(8,128)(2,1)S(1)}, bf16[12,1,192,128]{3,2,1,0:T(8,128)(2,1)}, u32[]{:S(2)}) copy-start(bf16[12,1,192,128]{3,2,1,0:T(8,128)(2,1)} %custom-call) | copy-start | bytes 1769476
  762.8 65.8 %copy-start.7 = (f32[1536]{0:T(1024)S(1)}, f32[1536]{0:T(1024)}, u32[]{:S(2)}) copy-start(f32[1536]{0:T(1024)} %get-tuple-element.101) | copy-start | bytes 18436
where the time goes:
time: 841 us; the launch traced here: 833 us
  waiting for transfers between devices  478 us (57%)
  local copies, waits for them, and re-layouts  189 us (22%)
  other arithmetic  79.2 us (9%)
  matrix products  69.1 us (8%)
  starting transfers between devices  17.3 us (2%)
    ppermute x3, waiting for transfers between devices, with_halo(): after = lax.ppermute(first, axis, down)  281 us
    ppermute x3, waiting for transfers between devices, with_halo(): before = lax.ppermute(last, axis, up)  197 us
    concatenate x3, other arithmetic, with_halo(): value = jnp.concatenate([before, value, after], axis=dim)  39.3 us
    unnamed x18, local copies, waits for them, and re-layouts  33.8 us
    another operation x1, local copies, waits for them, and re-layouts, one_row(): key_tiles.reshape(tile_columns, window, HEADS, HEAD_DIM)  29 us
    another operation x1, local copies, waits for them, and re-layouts, one_row(): value_tiles.reshape(tile_columns, window, HEADS, HEAD_DIM)  29 us
    dot_general x12, matrix products, one_head(): jnp.einsum('cqk,ckd->cqd', weights, head_value, preferred_element_type=jn...  28.2 us
    dot_general x12, matrix products, one_head(): jnp.einsum('cqd,ckd->cqk', head_query, head_key, preferred_element_type=j...  26 us
  transfers between devices with their start and end apart: 6, of which 6 were waited for; matrix products, arithmetic and copies ran while one was open for 3% of the time, Pallas kernels for 0%

commit v1 on v0

v1 whole, which is shorter than its diff:
```python
import jax
import jax.numpy as jnp
import numpy as np
from jax import lax
from jax.experimental import pallas as pl
from jax.experimental.pallas import tpu as pltpu
from jax.sharding import PartitionSpec as P

HEADS = 12
HD = 128
D = 1536
N = 192
CHUNK = 256
NCHUNK = D // CHUNK
SLOTS = 9
OWN, WD, WZ, SIB, SIB_WD, SIB_WZ, AC_WD, AC, AC_WZ = range(SLOTS)
AHEAD = 2
MESH = pl.DeviceIdType.MESH
F32 = jnp.float32
BF16 = jnp.bfloat16


def angle_tables():
    half, sixth = HD // 2, HD // 6
    first = half - 2 * sixth
    freq_first = 10000.0 ** (-np.arange(first) / first)
    freq_rest = 10000.0 ** (-np.arange(sixth) / sixth)
    table = np.zeros((16, 8, 3, HD))
    for base, groups, size, start, freq in (
        (0, 4, 3, 0, freq_first),
        (4, 4, 8, first, freq_rest),
        (8, 8, 8, first + sixth, freq_rest),
    ):
        for group in range(groups):
            for row in range(size):
                angle = (group * size + row) * freq
                lanes = 2 * (start + np.arange(len(freq)))
                table[base + group, row, 0, lanes] = np.cos(angle)
                table[base + group, row, 0, lanes + 1] = np.cos(angle)
                table[base + group, row, 1, lanes] = -np.sin(angle)
                table[base + group, row, 2, lanes + 1] = np.sin(angle)
    return table.reshape(16, 8, 3 * HD).astype(np.float32)


def kernel(
    tok_ref, mod_ref, nq_ref, nk_ref, tab_ref, wq_hbm, wk_hbm, wv_hbm, wo_hbm,
    out_ref,
    wq, wk, wv, wo, xn, proj, cs, kv, ones, q, o_send, o_recv, o_own, st_send, st_recv, st_own, att,
    w_sem, kv_send, kv_recv, q_send, q_recv, o_ssem, o_rsem, st_ssem, st_rsem,
):
    ta, ha, wa = lax.axis_index("ta"), lax.axis_index("ha"), lax.axis_index("wa")
    edge = lax.rem(wa, 2)
    step = 2 - 4 * edge
    z_to, z_from = wa + step, wa - step
    has_to = jnp.logical_and(z_to >= 0, z_to < 8)
    has_from = jnp.logical_and(z_from >= 0, z_from < 8)
    inner = jnp.logical_and(ha >= 1, ha <= 2)
    inner_to = jnp.logical_and(inner, has_to)
    inner_from = jnp.logical_and(inner, has_from)
    has_prev, has_next = ta > 0, ta < 3
    direct = wa + 1 - 2 * edge
    sib = ha + 1 - 2 * lax.rem(ha, 2)
    dev_wd = (ta, ha, direct)
    dev_sib = (ta, sib, wa)
    dev_ac = (ta, 3 - ha, direct)
    dev_to = (ta, ha, z_to)
    dev_from = (ta, ha, z_from)
    dev_prev = (ta - 1, ha, wa)
    dev_next = (ta + 1, ha, wa)

    weights = ((wk_hbm, wk), (wv_hbm, wv), (wq_hbm, wq), (wo_hbm, wo))

    def weight_copy(which, c):
        hbm, buf = weights[which]
        return pltpu.make_async_copy(
            hbm.at[:, pl.ds(pl.multiple_of(c * CHUNK, CHUNK), CHUNK)], buf.at[c], w_sem.at[which, c]
        )

    for which in range(4):
        for c in range(NCHUNK):
            weight_copy(which, c).start()

    barrier = pltpu.get_barrier_semaphore()

    def greet(device):
        pl.semaphore_signal(barrier, inc=1, device_id=device, device_id_type=MESH)

    greet(dev_wd)
    greet(dev_sib)
    pl.when(has_to)(lambda: greet(dev_to))
    pl.when(has_from)(lambda: greet(dev_from))
    pl.when(inner)(lambda: greet(dev_ac))
    pl.when(has_prev)(lambda: greet(dev_prev))
    pl.when(has_next)(lambda: greet(dev_next))

    tf, tr, tc = tab_ref[ta], tab_ref[4 + ha], tab_ref[8 + wa]
    for f in range(3):
        for r in range(8):
            cs[pl.ds((f * 8 + r) * 8, 8), :] = tc + tr[r : r + 1, :] + tf[f : f + 1, :]

    scale = 1.0 + mod_ref[1:2, :]
    shift = mod_ref[0:1, :]
    for r in range(N // 32):
        rows = pl.ds(r * 32, 32)
        values = tok_ref[rows, :].astype(F32)
        center = values - jnp.mean(values, axis=-1, keepdims=True)
        spread = jnp.mean(center * center, axis=-1, keepdims=True)
        xn[rows, :] = (center * lax.rsqrt(spread + 1e-6) * scale + shift).astype(BF16)

    def project(which, store):
        def one(c, total):
            weight_copy(which, c).wait()
            acc = jnp.dot(xn[...], weights[which][1][c], preferred_element_type=F32)
            return store(c, acc, total)

        return lax.fori_loop(0, NCHUNK, one, jnp.zeros((N, HD), F32))

    def keep(c, acc, total):
        left, right = acc[:, :HD], acc[:, HD:]
        proj[2 * c] = left
        proj[2 * c + 1] = right
        return total + left * left + right * right

    def store_value(c, acc, total):
        kv[OWN, 2 * c, :, HD:] = acc[:, :HD].astype(BF16)
        kv[OWN, 2 * c + 1, :, HD:] = acc[:, HD:].astype(BF16)
        return total

    def rotated(h, inv, gain_ref):
        x = proj[h] * inv * gain_ref[h]
        return (
            x * cs[:, :HD]
            + pltpu.roll(x, HD - 1, 1) * cs[:, HD : 2 * HD]
            + pltpu.roll(x, 1, 1) * cs[:, 2 * HD :]
        ).astype(BF16)

    def inverse(total):
        return lax.rsqrt(jnp.sum(total, axis=-1, keepdims=True) * (1.0 / D) + 1e-6)

    own_wd = (0, OWN, WD, dev_wd)
    own_sib = (1, OWN, SIB, dev_sib)
    own_ac = (2, OWN, AC_WD, dev_ac)
    wd_to = (3, WD, WZ, dev_to)
    wd_sib = (4, WD, SIB_WD, dev_sib)
    wd_ac = (5, WD, AC, dev_ac)
    ac_to = (6, AC_WD, AC_WZ, dev_to)
    wz_sib = (7, WZ, SIB_WZ, dev_sib)

    def flow(which, h):
        index, source, target, device = which
        return pltpu.make_async_remote_copy(
            src_ref=kv.at[source, h],
            dst_ref=kv.at[target, h],
            send_sem=kv_send.at[index, h],
            recv_sem=kv_recv.at[index, h],
            device_id=device,
            device_id_type=MESH,
        )

    value_total = project(1, store_value)
    inv_k = inverse(project(0, keep))

    partners = (
        2
        + has_to.astype(jnp.int32)
        + has_from.astype(jnp.int32)
        + inner.astype(jnp.int32)
        + has_prev.astype(jnp.int32)
        + has_next.astype(jnp.int32)
    )
    pl.semaphore_wait(barrier, partners)

    @pl.loop(0, HEADS)
    def _(h):
        kv[OWN, h, :, :HD] = rotated(h, inv_k, nk_ref)
        flow(own_wd, h).start()
        pl.when(inner)(lambda: flow(own_ac, h).start())
        flow(own_sib, h).start()

    def absent(slot):
        ones[slot] = jnp.zeros((N, HD), BF16)

        @pl.loop(0, HEADS)
        def _(h):
            kv[slot, h, :, :HD] = kv[OWN, h, :, :HD]
            kv[slot, h, :, HD:] = jnp.zeros((N, HD), BF16)

    for slot in range(SLOTS):
        ones[slot] = jnp.ones((N, HD), BF16)

    @pl.when(jnp.logical_not(has_from))
    def _():
        absent(WZ)
        absent(SIB_WZ)

    @pl.when(jnp.logical_not(inner))
    def _():
        absent(AC_WD)
        absent(AC)

    @pl.when(jnp.logical_not(inner_from))
    def _():
        absent(AC_WZ)

    @pl.when(jnp.logical_not(has_prev))
    def _():
        q[1] = jnp.zeros((HEADS, N, HD), BF16)
        o_recv[0] = jnp.zeros((HEADS, N, HD), BF16)
        st_recv[0] = jnp.full((N, HD), -1e30, F32)

    @pl.when(jnp.logical_not(has_next))
    def _():
        q[2] = jnp.zeros((HEADS, N, HD), BF16)
        o_recv[1] = jnp.zeros((HEADS, N, HD), BF16)
        st_recv[1] = jnp.full((N, HD), -1e30, F32)

    def query_flow(which, h):
        return pltpu.make_async_remote_copy(
            src_ref=q.at[0, h],
            dst_ref=q.at[1 + which, h],
            send_sem=q_send.at[which, h],
            recv_sem=q_recv.at[which, h],
            device_id=(dev_next, dev_prev)[which],
            device_id_type=MESH,
        )

    def result_flow(which, h):
        return pltpu.make_async_remote_copy(
            src_ref=o_send.at[which, h],
            dst_ref=o_recv.at[1 - which, h],
            send_sem=o_ssem.at[which, h],
            recv_sem=o_rsem.at[1 - which, h],
            device_id=(dev_prev, dev_next)[which],
            device_id_type=MESH,
        )

    def stat_flow(which):
        return pltpu.make_async_remote_copy(
            src_ref=st_send.at[which],
            dst_ref=st_recv.at[1 - which],
            send_sem=st_ssem.at[which],
            recv_sem=st_rsem.at[1 - which],
            device_id=(dev_prev, dev_next)[which],
            device_id_type=MESH,
        )

    inv_q = inverse(project(2, keep))

    @pl.loop(0, HEADS)
    def _(h):
        q[0, h] = rotated(h, inv_q, nq_ref)
        pl.when(has_next)(lambda: query_flow(0, h).start())
        pl.when(has_prev)(lambda: query_flow(1, h).start())

    def pass_on(h):
        flow(own_wd, h).wait_recv()
        pl.when(has_to)(lambda: flow(wd_to, h).start())
        pl.when(inner)(lambda: flow(wd_ac, h).start())
        flow(wd_sib, h).start()
        pl.when(inner)(lambda: flow(own_ac, h).wait_recv())
        pl.when(inner_to)(lambda: flow(ac_to, h).start())

    for h in range(AHEAD):
        pass_on(h)

    factor = HD ** (-0.5)
    lanes = lax.broadcasted_iota(jnp.int32, (N, HD), 1)
    st_send[...] = jnp.zeros((2, N, HD), F32)
    st_own[...] = jnp.zeros((N, HD), F32)

    @pl.loop(0, HEADS)
    def _(h):
        pl.when(h + AHEAD < HEADS)(lambda: pass_on(h + AHEAD))

        @pl.when(has_from)
        def _():
            flow(wd_to, h).wait_recv()
            flow(wz_sib, h).start()

        flow(own_sib, h).wait_recv()
        flow(wd_sib, h).wait_recv()
        pl.when(inner)(lambda: flow(wd_ac, h).wait_recv())
        pl.when(inner_from)(lambda: flow(ac_to, h).wait_recv())
        pl.when(has_from)(lambda: flow(wz_sib, h).wait_recv())
        pl.when(has_prev)(lambda: query_flow(0, h).wait_recv())
        pl.when(has_next)(lambda: query_flow(1, h).wait_recv())

        keys = kv[:, h, :, :HD].reshape(SLOTS * N, HD)
        values = jnp.concatenate(
            [kv[:, h, :, HD:].reshape(SLOTS * N, HD), ones[...].reshape(SLOTS * N, HD)], axis=1
        )
        for part in (1, 2, 0):
            scores = lax.dot_general(
                q[part, h], keys, (((1,), (1,)), ((), ())), preferred_element_type=F32
            )
            peak = jnp.max(scores, axis=-1, keepdims=True)
            expo = jnp.exp((scores - peak) * factor).astype(BF16)
            acc = jnp.dot(expo, values, preferred_element_type=F32)
            result = acc[:, :HD] / acc[:, HD:]
            stat = peak * factor + jnp.log(acc[:, HD:])
            if part == 0:
                o_own[h] = result
                st_own[...] = jnp.where(lanes == h, stat, st_own[...])
            else:
                o_send[part - 1, h] = result.astype(BF16)
                st_send[part - 1] = jnp.where(lanes == h, stat, st_send[part - 1])

        pl.when(has_prev)(lambda: result_flow(0, h).start())
        pl.when(has_next)(lambda: result_flow(1, h).start())

    pl.when(has_prev)(lambda: stat_flow(0).start())
    pl.when(has_next)(lambda: stat_flow(1).start())

    @pl.when(has_next)
    def _():
        stat_flow(0).wait_recv()

        @pl.loop(0, HEADS)
        def _(h):
            result_flow(0, h).wait_recv()

    @pl.when(has_prev)
    def _():
        stat_flow(1).wait_recv()

        @pl.loop(0, HEADS)
        def _(h):
            result_flow(1, h).wait_recv()

    top = jnp.maximum(jnp.maximum(st_recv[0], st_recv[1]), st_own[...])
    e_prev, e_next, e_own = jnp.exp(st_recv[0] - top), jnp.exp(st_recv[1] - top), jnp.exp(st_own[...] - top)
    total = 1.0 / (e_prev + e_next + e_own)
    e_prev, e_next, e_own = e_prev * total, e_next * total, e_own * total
    for h in range(HEADS):
        column = slice(h, h + 1)
        att[:, h * HD : (h + 1) * HD] = (
            e_own[:, column] * o_own[h]
            + e_prev[:, column] * o_recv[0, h].astype(F32)
            + e_next[:, column] * o_recv[1, h].astype(F32)
        ).astype(BF16)

    for c in range(NCHUNK):
        weight_copy(3, c).wait()
        columns = slice(c * CHUNK, (c + 1) * CHUNK)
        out_ref[:, columns] = (
            jnp.dot(att[...], wo[c], preferred_element_type=F32) * mod_ref[2:3, columns]
        ).astype(BF16)

    @pl.loop(0, HEADS)
    def _(h):
        flow(own_wd, h).wait_send()
        flow(own_sib, h).wait_send()
        flow(wd_sib, h).wait_send()

        @pl.when(inner)
        def _():
            flow(own_ac, h).wait_send()
            flow(wd_ac, h).wait_send()

        pl.when(has_to)(lambda: flow(wd_to, h).wait_send())
        pl.when(inner_to)(lambda: flow(ac_to, h).wait_send())
        pl.when(has_from)(lambda: flow(wz_sib, h).wait_send())

        @pl.when(has_next)
        def _():
            query_flow(0, h).wait_send()
            result_flow(1, h).wait_send()

        @pl.when(has_prev)
        def _():
            query_flow(1, h).wait_send()
            result_flow(0, h).wait_send()

    pl.when(has_prev)(lambda: stat_flow(0).wait_send())
    pl.when(has_next)(lambda: stat_flow(1).wait_send())


def body(tokens, modulation, w_query, w_key, w_value, w_out, norm_q, norm_k):
    vmem = pl.BlockSpec(memory_space=pltpu.VMEM)
    hbm = pl.BlockSpec(memory_space=pl.ANY)
    weight = pltpu.VMEM((NCHUNK, D, CHUNK), BF16)
    dma = pltpu.SemaphoreType.DMA
    result = pl.pallas_call(
        kernel,
        out_shape=jax.ShapeDtypeStruct((N, D), BF16),
        in_specs=[vmem] * 5 + [hbm] * 4,
        out_specs=vmem,
        scratch_shapes=[
            weight, weight, weight, weight,
            pltpu.VMEM((N, D), BF16),
            pltpu.VMEM((HEADS, N, HD), F32),
            pltpu.VMEM((N, 3 * HD), F32),
            pltpu.VMEM((SLOTS, HEADS, N, 2 * HD), BF16),
            pltpu.VMEM((SLOTS, N, HD), BF16),
            pltpu.VMEM((3, HEADS, N, HD), BF16),
            pltpu.VMEM((2, HEADS, N, HD), BF16),
            pltpu.VMEM((2, HEADS, N, HD), BF16),
            pltpu.VMEM((HEADS, N, HD), F32),
            pltpu.VMEM((2, N, HD), F32),
            pltpu.VMEM((2, N, HD), F32),
            pltpu.VMEM((N, HD), F32),
            pltpu.VMEM((N, D), BF16),
            dma((4, NCHUNK)),
            dma((8, HEADS)), dma((8, HEADS)),
            dma((2, HEADS)), dma((2, HEADS)),
            dma((2, HEADS)), dma((2, HEADS)),
            dma((2,)), dma((2,)),
        ],
        compiler_params=pltpu.CompilerParams(
            collective_id=0, has_side_effects=True, vmem_limit_bytes=60 * 1024 * 1024
        ),
        name="tile_attention",
    )(
        tokens.reshape(N, D),
        modulation,
        norm_q.reshape(HEADS, 1, HD),
        norm_k.reshape(HEADS, 1, HD),
        jnp.asarray(angle_tables()),
        w_query, w_key, w_value, w_out,
    )
    return result.reshape(3, 8, 8, D)


def solution(mesh):
    in_specs = (P("ta", "ha", "wa", None), P(), P(), P(), P(), P(), P(), P())
    out_specs = P("ta", "ha", "wa", None)
    return jax.shard_map(body, mesh=mesh, in_specs=in_specs, out_specs=out_specs, check_vma=False)
```

time: 841 us -> 78.7 us (0.09)
  waiting for transfers between devices: 478 us -> 0 us
  local copies, waits for them, and re-layouts: 189 us -> 4.52 us
  other arithmetic: 79.2 us -> 0 us
  Pallas kernels: 0 us -> 73.4 us
  matrix products: 69.1 us -> 0 us
  starting transfers between devices: 17.3 us -> 0 us
    ppermute x6 -> x0, waiting for transfers between devices: 478 us -> none  [the longest x3 281 us: with_halo(): after = lax.ppermute(first, axis, down)]
    another operation x6 -> x0, local copies, waits for them, and re-layouts: 92.1 us -> none  [the longest x1 29 us: one_row(): key_tiles.reshape(tile_columns, window, HEADS, HEAD_DIM)]
    pallas_call x0 -> x1, Pallas kernels: none -> 73.4 us  [body(): pl.pallas_call(kernel, out_shape=jax.ShapeDtypeStruct((N, D), BF16), in_s...]
    dot_general x28 -> x0, matrix products: 69.1 us -> none  [the longest x12 28.2 us: one_head(): jnp.einsum('cqk,ckd->cqd', weights, head_value, preferred_element_type=jn...]
    concatenate x3 -> x0, other arithmetic: 39.3 us -> none  [with_halo(): value = jnp.concatenate([before, value, after], axis=dim)]
    unnamed x18 -> x1, local copies, waits for them, and re-layouts: 33.8 us -> 1.92 us
    slice x1 -> x0, local copies, waits for them, and re-layouts: 22 us -> none  [body(): attended = tile_rows(query, padded[0], padded[1], anchor, extent)]
    sub x1 -> x0, other arithmetic: 20.9 us -> none  [rotate_pairs(): even_part * cosine - odd_part * sine]
  transfers between devices with their start and end apart: 6 -> 0, of which waited for: 6 -> 0; matrix products, arithmetic and copies ran while one was open for 3% -> 0% of each run, Pallas kernels for 0% -> 0%
where the time goes in v1:
time: 78.7 us; the launch traced here: 77.9 us
  Pallas kernels  73.4 us (93%)
  local copies, waits for them, and re-layouts  4.52 us (6%)
    pallas_call x1, Pallas kernels, body(): pl.pallas_call(kernel, out_shape=jax.ShapeDtypeStruct((N, D), BF16), in_s...  73.4 us
    unnamed x1, local copies, waits for them, and re-layouts  1.92 us

profile of v1, /device:TPU:90, one launch (start us, length us, event | category | flops | bytes accessed | tf_op | source)
XLA Modules:
  0.0 77.9 jit_solution(1504008436754420579)
XLA Ops:
  0.0 1.3 %reshape.13.nq_ref = f32[12,1,128]{2,1,0:T(1,128)} reshape(f32[1536]{0:T(1024)} %param.15) | data formatting | bytes 12288 | tf_op jit(solution)/shard_map/reshape | solution.py:416
  1.3 1.3 %reshape.14.nk_ref = f32[12,1,128]{2,1,0:T(1,128)} reshape(f32[1536]{0:T(1024)} %param.16) | data formatting | bytes 12288 | tf_op jit(solution)/shard_map/reshape | solution.py:417
  2.6 73.4 %tile_attention.1 = bf16[192,1536]{1,0:T(8,128)(2,1)} custom-call(bf16[192,1536]{1,0:T(8,128)(2,1)} %bitcast.3, f32[3,1536]{1,0:T(4,128)} %mod_ref.1, f32[12,1,128]{2,1,0:T(1,128)} %reshape.13.nq_ref, f32[12,1,128]{2,1,0:T(1,128)} %reshape.14.nk_ref, f32[16,8,384]{2,1,0:T(8,128)} %constant.2.clone.tab_ref, bf16[1536,1536]{1,0:T(8,128)(2,1)} %wq_hbm.1, ...), custom_call_target="tpu_custom_call" | custom-call | tf_op jit(solution)/shard_map/tile_attention/pallas_call | solution.py:383
  76.0 1.9 %copy.11 = bf16[3,8,8,1536]{3,2,1,0:T(8,128)(2,1)} copy(bf16[3,8,8,1536]{3,2,1,0:T(8,128)(2,1)} %bitcast.2) | data formatting | bytes 1179648

commit v2 on v1

--- a/solution.py
+++ b/solution.py
@@ -15,6 +15,7 @@
 SLOTS = 9
 OWN, WD, WZ, SIB, SIB_WD, SIB_WZ, AC_WD, AC, AC_WZ = range(SLOTS)
 AHEAD = 2
+ROUND, TURN = 6, 3
 MESH = pl.DeviceIdType.MESH
 F32 = jnp.float32
 BF16 = jnp.bfloat16
@@ -45,8 +46,8 @@
 def kernel(
     tok_ref, mod_ref, nq_ref, nk_ref, tab_ref, wq_hbm, wk_hbm, wv_hbm, wo_hbm,
     out_ref,
-    wq, wk, wv, wo, xn, proj, cs, kv, ones, q, o_send, o_recv, o_own, st_send, st_recv, st_own, att,
-    w_sem, kv_send, kv_recv, q_send, q_recv, o_ssem, o_rsem, st_ssem, st_rsem,
+    wq, wk, wv, wo, xn, proj, cs, kv, transit, ones, q, o_send, o_recv, o_own, st_send, st_recv, st_parts, att,
+    w_sem, kv_send, kv_recv, tr_send, tr_recv, q_send, q_recv, o_ssem, o_rsem, st_ssem, st_rsem,
 ):
     ta, ha, wa = lax.axis_index("ta"), lax.axis_index("ha"), lax.axis_index("wa")
     edge = lax.rem(wa, 2)
@@ -121,13 +122,8 @@
         proj[2 * c + 1] = right
         return total + left * left + right * right
 
-    def store_value(c, acc, total):
-        kv[OWN, 2 * c, :, HD:] = acc[:, :HD].astype(BF16)
-        kv[OWN, 2 * c + 1, :, HD:] = acc[:, HD:].astype(BF16)
-        return total
-
     def rotated(h, inv, gain_ref):
-        x = proj[h] * inv * gain_ref[h]
+        x = proj[h] * inv * gain_ref[pl.ds(pl.multiple_of(h * HD, HD), HD)].reshape(1, HD)
         return (
             x * cs[:, :HD]
             + pltpu.roll(x, HD - 1, 1) * cs[:, HD : 2 * HD]
@@ -157,7 +153,22 @@
             device_id_type=MESH,
         )
 
-    value_total = project(1, store_value)
+    def turned(h):
+        return h % ROUND == TURN
+
+    def turn_flow(leg, h):
+        k = h // ROUND
+        source = kv.at[OWN, h] if leg == 0 else transit.at[k]
+        target = (transit.at[k], kv.at[WZ, h], kv.at[AC_WZ, h])[leg]
+        return pltpu.make_async_remote_copy(
+            src_ref=source,
+            dst_ref=target,
+            send_sem=tr_send.at[leg, k],
+            recv_sem=tr_recv.at[leg, k],
+            device_id=(dev_from, dev_wd, dev_ac)[leg],
+            device_id_type=MESH,
+        )
+
     inv_k = inverse(project(0, keep))
 
     partners = (
@@ -170,12 +181,18 @@
     )
     pl.semaphore_wait(barrier, partners)
 
-    @pl.loop(0, HEADS)
-    def _(h):
-        kv[OWN, h, :, :HD] = rotated(h, inv_k, nk_ref)
-        flow(own_wd, h).start()
-        pl.when(inner)(lambda: flow(own_ac, h).start())
-        flow(own_sib, h).start()
+    def store_and_send(c, acc, total):
+        for half in range(2):
+            h = 2 * c + half
+            kv[OWN, h, :, HD:] = acc[:, half * HD : (half + 1) * HD].astype(BF16)
+            kv[OWN, h, :, :HD] = rotated(h, inv_k, nk_ref)
+            flow(own_wd, h).start()
+            pl.when(inner)(lambda: flow(own_ac, h).start())
+            flow(own_sib, h).start()
+            pl.when(jnp.logical_and(has_from, turned(h)))(lambda: turn_flow(0, h).start())
+        return total
+
+    project(1, store_and_send)
 
     def absent(slot):
         ones[slot] = jnp.zeros((N, HD), BF16)
@@ -206,13 +223,13 @@
     def _():
         q[1] = jnp.zeros((HEADS, N, HD), BF16)
         o_recv[0] = jnp.zeros((HEADS, N, HD), BF16)
-        st_recv[0] = jnp.full((N, HD), -1e30, F32)
+        st_recv[0] = jnp.full((16, 256), -1e30, F32)
 
     @pl.when(jnp.logical_not(has_next))
     def _():
         q[2] = jnp.zeros((HEADS, N, HD), BF16)
         o_recv[1] = jnp.zeros((HEADS, N, HD), BF16)
-        st_recv[1] = jnp.full((N, HD), -1e30, F32)
+        st_recv[1] = jnp.full((16, 256), -1e30, F32)
 
     def query_flow(which, h):
         return pltpu.make_async_remote_copy(
@@ -254,33 +271,45 @@
 
     def pass_on(h):
         flow(own_wd, h).wait_recv()
-        pl.when(has_to)(lambda: flow(wd_to, h).start())
+        turn = turned(h)
+        straight = jnp.logical_not(turn)
+        pl.when(jnp.logical_and(has_to, straight))(lambda: flow(wd_to, h).start())
         pl.when(inner)(lambda: flow(wd_ac, h).start())
         flow(wd_sib, h).start()
         pl.when(inner)(lambda: flow(own_ac, h).wait_recv())
-        pl.when(inner_to)(lambda: flow(ac_to, h).start())
+        pl.when(jnp.logical_and(inner_to, straight))(lambda: flow(ac_to, h).start())
+
+        @pl.when(jnp.logical_and(has_to, turn))
+        def _():
+            turn_flow(0, h).wait_recv()
+            turn_flow(1, h).start()
+            pl.when(inner)(lambda: turn_flow(2, h).start())
 
     for h in range(AHEAD):
         pass_on(h)
 
     factor = HD ** (-0.5)
     lanes = lax.broadcasted_iota(jnp.int32, (N, HD), 1)
-    st_send[...] = jnp.zeros((2, N, HD), F32)
-    st_own[...] = jnp.zeros((N, HD), F32)
+    st_parts[...] = jnp.zeros((3, 256, HD), F32)
 
     @pl.loop(0, HEADS)
     def _(h):
         pl.when(h + AHEAD < HEADS)(lambda: pass_on(h + AHEAD))
 
+        turn = turned(h)
+        straight = jnp.logical_not(turn)
+
         @pl.when(has_from)
         def _():
-            flow(wd_to, h).wait_recv()
+            pl.when(straight)(lambda: flow(wd_to, h).wait_recv())
+            pl.when(turn)(lambda: turn_flow(1, h).wait_recv())
             flow(wz_sib, h).start()
 
         flow(own_sib, h).wait_recv()
         flow(wd_sib, h).wait_recv()
         pl.when(inner)(lambda: flow(wd_ac, h).wait_recv())
-        pl.when(inner_from)(lambda: flow(ac_to, h).wait_recv())
+        pl.when(jnp.logical_and(inner_from, straight))(lambda: flow(ac_to, h).wait_recv())
+        pl.when(jnp.logical_and(inner_from, turn))(lambda: turn_flow(2, h).wait_recv())
         pl.when(has_from)(lambda: flow(wz_sib, h).wait_recv())
         pl.when(has_prev)(lambda: query_flow(0, h).wait_recv())
         pl.when(has_next)(lambda: query_flow(1, h).wait_recv())
@@ -289,25 +318,25 @@
         values = jnp.concatenate(
             [kv[:, h, :, HD:].reshape(SLOTS * N, HD), ones[...].reshape(SLOTS * N, HD)], axis=1
         )
-        for part in (1, 2, 0):
+        def attend(part):
             scores = lax.dot_general(
                 q[part, h], keys, (((1,), (1,)), ((), ())), preferred_element_type=F32
             )
             peak = jnp.max(scores, axis=-1, keepdims=True)
             expo = jnp.exp((scores - peak) * factor).astype(BF16)
             acc = jnp.dot(expo, values, preferred_element_type=F32)
-            result = acc[:, :HD] / acc[:, HD:]
             stat = peak * factor + jnp.log(acc[:, HD:])
-            if part == 0:
-                o_own[h] = result
-                st_own[...] = jnp.where(lanes == h, stat, st_own[...])
-            else:
-                o_send[part - 1, h] = result.astype(BF16)
-                st_send[part - 1] = jnp.where(lanes == h, stat, st_send[part - 1])
-
+            st_parts[part, :N] = jnp.where(lanes == h, stat, st_parts[part, :N])
+            return acc[:, :HD] / acc[:, HD:]
+
+        for part in (1, 2):
+            o_send[part - 1, h] = attend(part).astype(BF16)
         pl.when(has_prev)(lambda: result_flow(0, h).start())
         pl.when(has_next)(lambda: result_flow(1, h).start())
-
+        o_own[h] = attend(0)
+
+    for which in range(2):
+        st_send[which] = jnp.transpose(st_parts[1 + which])[:16]
     pl.when(has_prev)(lambda: stat_flow(0).start())
     pl.when(has_next)(lambda: stat_flow(1).start())
 
@@ -327,8 +356,12 @@
         def _(h):
             result_flow(1, h).wait_recv()
 
-    top = jnp.maximum(jnp.maximum(st_recv[0], st_recv[1]), st_own[...])
-    e_prev, e_next, e_own = jnp.exp(st_recv[0] - top), jnp.exp(st_recv[1] - top), jnp.exp(st_own[...] - top)
+    below = jnp.zeros((HD - 16, 256), F32)
+    l_prev = jnp.transpose(jnp.concatenate([st_recv[0], below], axis=0))[:N]
+    l_next = jnp.transpose(jnp.concatenate([st_recv[1], below], axis=0))[:N]
+    l_own = st_parts[0, :N]
+    top = jnp.maximum(jnp.maximum(l_prev, l_next), l_own)
+    e_prev, e_next, e_own = jnp.exp(l_prev - top), jnp.exp(l_next - top), jnp.exp(l_own - top)
     total = 1.0 / (e_prev + e_next + e_own)
     e_prev, e_next, e_own = e_prev * total, e_next * total, e_own * total
     for h in range(HEADS):
@@ -357,8 +390,13 @@
             flow(own_ac, h).wait_send()
             flow(wd_ac, h).wait_send()
 
-        pl.when(has_to)(lambda: flow(wd_to, h).wait_send())
-        pl.when(inner_to)(lambda: flow(ac_to, h).wait_send())
+        turn = turned(h)
+        straight = jnp.logical_not(turn)
+        pl.when(jnp.logical_and(has_to, straight))(lambda: flow(wd_to, h).wait_send())
+        pl.when(jnp.logical_and(inner_to, straight))(lambda: flow(ac_to, h).wait_send())
+        pl.when(jnp.logical_and(has_from, turn))(lambda: turn_flow(0, h).wait_send())
+        pl.when(jnp.logical_and(has_to, turn))(lambda: turn_flow(1, h).wait_send())
+        pl.when(jnp.logical_and(inner_to, turn))(lambda: turn_flow(2, h).wait_send())
         pl.when(has_from)(lambda: flow(wz_sib, h).wait_send())
 
         @pl.when(has_next)
@@ -391,17 +429,19 @@
             pltpu.VMEM((HEADS, N, HD), F32),
             pltpu.VMEM((N, 3 * HD), F32),
             pltpu.VMEM((SLOTS, HEADS, N, 2 * HD), BF16),
+            pltpu.VMEM((HEADS // ROUND, N, 2 * HD), BF16),
             pltpu.VMEM((SLOTS, N, HD), BF16),
             pltpu.VMEM((3, HEADS, N, HD), BF16),
             pltpu.VMEM((2, HEADS, N, HD), BF16),
             pltpu.VMEM((2, HEADS, N, HD), BF16),
             pltpu.VMEM((HEADS, N, HD), F32),
-            pltpu.VMEM((2, N, HD), F32),
-            pltpu.VMEM((2, N, HD), F32),
-            pltpu.VMEM((N, HD), F32),
+            pltpu.VMEM((2, 16, 256), F32),
+            pltpu.VMEM((2, 16, 256), F32),
+            pltpu.VMEM((3, 256, HD), F32),
             pltpu.VMEM((N, D), BF16),
             dma((4, NCHUNK)),
             dma((8, HEADS)), dma((8, HEADS)),
+            dma((3, HEADS // ROUND)), dma((3, HEADS // ROUND)),
             dma((2, HEADS)), dma((2, HEADS)),
             dma((2, HEADS)), dma((2, HEADS)),
             dma((2,)), dma((2,)),
@@ -413,8 +453,8 @@
     )(
         tokens.reshape(N, D),
         modulation,
-        norm_q.reshape(HEADS, 1, HD),
-        norm_k.reshape(HEADS, 1, HD),
+        norm_q,
+        norm_k,
         jnp.asarray(angle_tables()),
         w_query, w_key, w_value, w_out,
     )

time: 78.7 us -> 80.3 us (1.020)
  Pallas kernels: 73.4 us -> 76.9 us
  local copies, waits for them, and re-layouts: 4.52 us -> 1.92 us
    pallas_call x1, Pallas kernels: 73.4 us -> 76.9 us  [body(): pl.pallas_call(kernel, out_shape=jax.ShapeDtypeStruct((N, D), BF16), in_s...]
    reshape x2 -> x0, local copies, waits for them, and re-layouts: 2.6 us -> none  [the longest x1 1.3 us: body(): norm_k.reshape(HEADS, 1, HD)]
where the time goes in v2:
time: 80.3 us; the launch traced here: 78.8 us
  Pallas kernels  76.9 us (96%)
  local copies, waits for them, and re-layouts  1.92 us (2%)
    pallas_call x1, Pallas kernels, body(): pl.pallas_call(kernel, out_shape=jax.ShapeDtypeStruct((N, D), BF16), in_s...  76.9 us
    unnamed x1, local copies, waits for them, and re-layouts  1.92 us

profile of v2, /device:TPU:90, one launch (start us, length us, event | category | flops | bytes accessed | tf_op | source)
XLA Modules:
  0.0 78.8 jit_solution(1462284185796200421)
XLA Ops:
  0.0 76.9 %tile_attention.1 = bf16[192,1536]{1,0:T(8,128)(2,1)} custom-call(bf16[192,1536]{1,0:T(8,128)(2,1)} %bitcast.3, f32[3,1536]{1,0:T(4,128)} %mod_ref.1, f32[1536]{0:T(1024)} %nq_ref.1, f32[1536]{0:T(1024)} %nk_ref.1, f32[16,8,384]{2,1,0:T(8,128)} %constant.2.clone.tab_ref, bf16[1536,1536]{1,0:T(8,128)(2,1)} %wq_hbm.1, bf16[1536,1536]{1,0:T(8,128)(2,1)} %wk_hbm.1, ...), custom_call_target="tpu_custom_call" | custom-call | tf_op jit(solution)/shard_map/tile_attention/pallas_call | solution.py:421
  76.9 1.9 %copy.11 = bf16[3,8,8,1536]{3,2,1,0:T(8,128)(2,1)} copy(bf16[3,8,8,1536]{3,2,1,0:T(8,128)(2,1)} %bitcast.2) | data formatting | bytes 1179648

commit v3 on v2

--- a/solution.py
+++ b/solution.py
@@ -14,8 +14,10 @@
 NCHUNK = D // CHUNK
 SLOTS = 9
 OWN, WD, WZ, SIB, SIB_WD, SIB_WZ, AC_WD, AC, AC_WZ = range(SLOTS)
-AHEAD = 2
-ROUND, TURN = 6, 3
+AHEAD = 3
+SHARE = 1
+AT_ONCE = 4
+TURN = 8
 MESH = pl.DeviceIdType.MESH
 F32 = jnp.float32
 BF16 = jnp.bfloat16
@@ -154,10 +156,10 @@
         )
 
     def turned(h):
-        return h % ROUND == TURN
+        return jnp.logical_and(h >= TURN, h % 2 == 0)
 
     def turn_flow(leg, h):
-        k = h // ROUND
+        k = (h - TURN) // 2
         source = kv.at[OWN, h] if leg == 0 else transit.at[k]
         target = (transit.at[k], kv.at[WZ, h], kv.at[AC_WZ, h])[leg]
         return pltpu.make_async_remote_copy(
@@ -187,7 +189,7 @@
             kv[OWN, h, :, HD:] = acc[:, half * HD : (half + 1) * HD].astype(BF16)
             kv[OWN, h, :, :HD] = rotated(h, inv_k, nk_ref)
             flow(own_wd, h).start()
-            pl.when(inner)(lambda: flow(own_ac, h).start())
+            pl.when(jnp.logical_and(inner, h < AT_ONCE))(lambda: flow(own_ac, h).start())
             flow(own_sib, h).start()
             pl.when(jnp.logical_and(has_from, turned(h)))(lambda: turn_flow(0, h).start())
         return total
@@ -274,6 +276,7 @@
         turn = turned(h)
         straight = jnp.logical_not(turn)
         pl.when(jnp.logical_and(has_to, straight))(lambda: flow(wd_to, h).start())
+        pl.when(jnp.logical_and(inner, h + AT_ONCE < HEADS))(lambda: flow(own_ac, h + AT_ONCE).start())
         pl.when(inner)(lambda: flow(wd_ac, h).start())
         flow(wd_sib, h).start()
         pl.when(inner)(lambda: flow(own_ac, h).wait_recv())
@@ -285,8 +288,19 @@
             turn_flow(1, h).start()
             pl.when(inner)(lambda: turn_flow(2, h).start())
 
+    def share(h):
+        turn = turned(h)
+
+        @pl.when(has_from)
+        def _():
+            pl.when(jnp.logical_not(turn))(lambda: flow(wd_to, h).wait_recv())
+            pl.when(turn)(lambda: turn_flow(1, h).wait_recv())
+            flow(wz_sib, h).start()
+
     for h in range(AHEAD):
         pass_on(h)
+    for h in range(SHARE):
+        share(h)
 
     factor = HD ** (-0.5)
     lanes = lax.broadcasted_iota(jnp.int32, (N, HD), 1)
@@ -296,15 +310,9 @@
     def _(h):
         pl.when(h + AHEAD < HEADS)(lambda: pass_on(h + AHEAD))
 
+        pl.when(h + SHARE < HEADS)(lambda: share(h + SHARE))
         turn = turned(h)
         straight = jnp.logical_not(turn)
-
-        @pl.when(has_from)
-        def _():
-            pl.when(straight)(lambda: flow(wd_to, h).wait_recv())
-            pl.when(turn)(lambda: turn_flow(1, h).wait_recv())
-            flow(wz_sib, h).start()
-
         flow(own_sib, h).wait_recv()
         flow(wd_sib, h).wait_recv()
         pl.when(inner)(lambda: flow(wd_ac, h).wait_recv())
@@ -429,7 +437,7 @@
             pltpu.VMEM((HEADS, N, HD), F32),
             pltpu.VMEM((N, 3 * HD), F32),
             pltpu.VMEM((SLOTS, HEADS, N, 2 * HD), BF16),
-            pltpu.VMEM((HEADS // ROUND, N, 2 * HD), BF16),
+            pltpu.VMEM(((HEADS - TURN) // 2, N, 2 * HD), BF16),
             pltpu.VMEM((SLOTS, N, HD), BF16),
             pltpu.VMEM((3, HEADS, N, HD), BF16),
             pltpu.VMEM((2, HEADS, N, HD), BF16),
@@ -441,7 +449,7 @@
             pltpu.VMEM((N, D), BF16),
             dma((4, NCHUNK)),
             dma((8, HEADS)), dma((8, HEADS)),
-            dma((3, HEADS // ROUND)), dma((3, HEADS // ROUND)),
+            dma((3, (HEADS - TURN) // 2)), dma((3, (HEADS - TURN) // 2)),
             dma((2, HEADS)), dma((2, HEADS)),
             dma((2, HEADS)), dma((2, HEADS)),
             dma((2,)), dma((2,)),

time: 80.3 us -> 69.6 us (0.87); the launches traced: 78.8 us -> 69.5 us
  Pallas kernels: 76.9 us -> 67.5 us
    pallas_call x1, Pallas kernels: 76.9 us -> 67.5 us  [body(): pl.pallas_call(kernel, out_shape=jax.ShapeDtypeStruct((N, D), BF16), in_s...]
where the time goes in v3:
time: 69.6 us; the launch traced here: 69.5 us
  Pallas kernels  67.5 us (97%)
  local copies, waits for them, and re-layouts  1.92 us (3%)
    pallas_call x1, Pallas kernels, body(): pl.pallas_call(kernel, out_shape=jax.ShapeDtypeStruct((N, D), BF16), in_s...  67.5 us
    unnamed x1, local copies, waits for them, and re-layouts  1.92 us

profile of v3, /device:TPU:90, one launch (start us, length us, event | category | flops | bytes accessed | tf_op | source)
XLA Modules:
  0.0 69.5 jit_solution(15972485340648254830)
XLA Ops:
  0.0 67.5 %tile_attention.1 = bf16[192,1536]{1,0:T(8,128)(2,1)} custom-call(bf16[192,1536]{1,0:T(8,128)(2,1)} %bitcast.3, f32[3,1536]{1,0:T(4,128)} %mod_ref.1, f32[1536]{0:T(1024)} %nq_ref.1, f32[1536]{0:T(1024)} %nk_ref.1, f32[16,8,384]{2,1,0:T(8,128)} %constant.2.clone.tab_ref, bf16[1536,1536]{1,0:T(8,128)(2,1)} %wq_hbm.1, bf16[1536,1536]{1,0:T(8,128)(2,1)} %wk_hbm.1, ...), custom_call_target="tpu_custom_call" | custom-call | tf_op jit(solution)/shard_map/tile_attention/pallas_call | solution.py:429
  67.5 1.9 %copy.11 = bf16[3,8,8,1536]{3,2,1,0:T(8,128)(2,1)} copy(bf16[3,8,8,1536]{3,2,1,0:T(8,128)(2,1)} %bitcast.2) | data formatting | bytes 1179648

commit v4 on v3

--- a/solution.py
+++ b/solution.py
@@ -18,6 +18,8 @@
 SHARE = 1
 AT_ONCE = 4
 TURN = 8
+AC_TURN = 4
+EARLY = 10
 MESH = pl.DeviceIdType.MESH
 F32 = jnp.float32
 BF16 = jnp.bfloat16
@@ -158,8 +160,14 @@
     def turned(h):
         return jnp.logical_and(h >= TURN, h % 2 == 0)
 
+    def ac_turned(h):
+        return jnp.logical_and(h >= AC_TURN, h % 2 == 0)
+
+    def in_transit(h):
+        return jnp.logical_or(turned(h), jnp.logical_and(inner, ac_turned(h)))
+
     def turn_flow(leg, h):
-        k = (h - TURN) // 2
+        k = (h - AC_TURN) // 2
         source = kv.at[OWN, h] if leg == 0 else transit.at[k]
         target = (transit.at[k], kv.at[WZ, h], kv.at[AC_WZ, h])[leg]
         return pltpu.make_async_remote_copy(
@@ -191,7 +199,7 @@
             flow(own_wd, h).start()
             pl.when(jnp.logical_and(inner, h < AT_ONCE))(lambda: flow(own_ac, h).start())
             flow(own_sib, h).start()
-            pl.when(jnp.logical_and(has_from, turned(h)))(lambda: turn_flow(0, h).start())
+            pl.when(jnp.logical_and(has_from, in_transit(h)))(lambda: turn_flow(0, h).start())
         return total
 
     project(1, store_and_send)
@@ -225,13 +233,13 @@
     def _():
         q[1] = jnp.zeros((HEADS, N, HD), BF16)
         o_recv[0] = jnp.zeros((HEADS, N, HD), BF16)
-        st_recv[0] = jnp.full((16, 256), -1e30, F32)
+        st_recv[:, 0] = jnp.full((2, 16, 256), -1e30, F32)
 
     @pl.when(jnp.logical_not(has_next))
     def _():
         q[2] = jnp.zeros((HEADS, N, HD), BF16)
         o_recv[1] = jnp.zeros((HEADS, N, HD), BF16)
-        st_recv[1] = jnp.full((16, 256), -1e30, F32)
+        st_recv[:, 1] = jnp.full((2, 16, 256), -1e30, F32)
 
     def query_flow(which, h):
         return pltpu.make_async_remote_copy(
@@ -253,12 +261,12 @@
             device_id_type=MESH,
         )
 
-    def stat_flow(which):
+    def stat_flow(stage, which):
         return pltpu.make_async_remote_copy(
-            src_ref=st_send.at[which],
-            dst_ref=st_recv.at[1 - which],
-            send_sem=st_ssem.at[which],
-            recv_sem=st_rsem.at[1 - which],
+            src_ref=st_send.at[stage, which],
+            dst_ref=st_recv.at[stage, 1 - which],
+            send_sem=st_ssem.at[stage, which],
+            recv_sem=st_rsem.at[stage, 1 - which],
             device_id=(dev_prev, dev_next)[which],
             device_id_type=MESH,
         )
@@ -273,20 +281,19 @@
 
     def pass_on(h):
         flow(own_wd, h).wait_recv()
-        turn = turned(h)
-        straight = jnp.logical_not(turn)
-        pl.when(jnp.logical_and(has_to, straight))(lambda: flow(wd_to, h).start())
+        turn, ac_turn = turned(h), ac_turned(h)
+        pl.when(jnp.logical_and(has_to, jnp.logical_not(turn)))(lambda: flow(wd_to, h).start())
         pl.when(jnp.logical_and(inner, h + AT_ONCE < HEADS))(lambda: flow(own_ac, h + AT_ONCE).start())
         pl.when(inner)(lambda: flow(wd_ac, h).start())
         flow(wd_sib, h).start()
         pl.when(inner)(lambda: flow(own_ac, h).wait_recv())
-        pl.when(jnp.logical_and(inner_to, straight))(lambda: flow(ac_to, h).start())
-
-        @pl.when(jnp.logical_and(has_to, turn))
+        pl.when(jnp.logical_and(inner_to, jnp.logical_not(ac_turn)))(lambda: flow(ac_to, h).start())
+
+        @pl.when(jnp.logical_and(has_to, in_transit(h)))
         def _():
             turn_flow(0, h).wait_recv()
-            turn_flow(1, h).start()
-            pl.when(inner)(lambda: turn_flow(2, h).start())
+            pl.when(turn)(lambda: turn_flow(1, h).start())
+            pl.when(jnp.logical_and(inner, ac_turn))(lambda: turn_flow(2, h).start())
 
     def share(h):
         turn = turned(h)
@@ -302,22 +309,25 @@
     for h in range(SHARE):
         share(h)
 
-    factor = HD ** (-0.5)
+    factor = HD ** (-0.5) * float(np.log2(np.e))
     lanes = lax.broadcasted_iota(jnp.int32, (N, HD), 1)
     st_parts[...] = jnp.zeros((3, 256, HD), F32)
 
+    def send_stats(stage):
+        for which, has in ((0, has_prev), (1, has_next)):
+            st_send[stage, which] = jnp.transpose(st_parts[1 + which])[:16]
+            pl.when(has)(lambda: stat_flow(stage, which).start())
+
     @pl.loop(0, HEADS)
     def _(h):
-        pl.when(h + AHEAD < HEADS)(lambda: pass_on(h + AHEAD))
-
-        pl.when(h + SHARE < HEADS)(lambda: share(h + SHARE))
-        turn = turned(h)
-        straight = jnp.logical_not(turn)
+        ahead = AHEAD + h + h // 2
+        pl.when(ahead < HEADS)(lambda: pass_on(ahead))
+        ac_turn = ac_turned(h)
         flow(own_sib, h).wait_recv()
         flow(wd_sib, h).wait_recv()
         pl.when(inner)(lambda: flow(wd_ac, h).wait_recv())
-        pl.when(jnp.logical_and(inner_from, straight))(lambda: flow(ac_to, h).wait_recv())
-        pl.when(jnp.logical_and(inner_from, turn))(lambda: turn_flow(2, h).wait_recv())
+        pl.when(jnp.logical_and(inner_from, jnp.logical_not(ac_turn)))(lambda: flow(ac_to, h).wait_recv())
+        pl.when(jnp.logical_and(inner_from, ac_turn))(lambda: turn_flow(2, h).wait_recv())
         pl.when(has_from)(lambda: flow(wz_sib, h).wait_recv())
         pl.when(has_prev)(lambda: query_flow(0, h).wait_recv())
         pl.when(has_next)(lambda: query_flow(1, h).wait_recv())
@@ -331,9 +341,9 @@
                 q[part, h], keys, (((1,), (1,)), ((), ())), preferred_element_type=F32
             )
             peak = jnp.max(scores, axis=-1, keepdims=True)
-            expo = jnp.exp((scores - peak) * factor).astype(BF16)
+            expo = jnp.exp2((scores - peak) * factor).astype(BF16)
             acc = jnp.dot(expo, values, preferred_element_type=F32)
-            stat = peak * factor + jnp.log(acc[:, HD:])
+            stat = peak * factor + jnp.log2(acc[:, HD:])
             st_parts[part, :N] = jnp.where(lanes == h, stat, st_parts[part, :N])
             return acc[:, :HD] / acc[:, HD:]
 
@@ -341,50 +351,55 @@
             o_send[part - 1, h] = attend(part).astype(BF16)
         pl.when(has_prev)(lambda: result_flow(0, h).start())
         pl.when(has_next)(lambda: result_flow(1, h).start())
+        pl.when(h + SHARE < HEADS)(lambda: share(h + SHARE))
+        pl.when(jnp.logical_and(h % 2 == 1, ahead + 1 < HEADS))(lambda: pass_on(ahead + 1))
         o_own[h] = attend(0)
 
-    for which in range(2):
-        st_send[which] = jnp.transpose(st_parts[1 + which])[:16]
-    pl.when(has_prev)(lambda: stat_flow(0).start())
-    pl.when(has_next)(lambda: stat_flow(1).start())
-
-    @pl.when(has_next)
-    def _():
-        stat_flow(0).wait_recv()
-
-        @pl.loop(0, HEADS)
-        def _(h):
-            result_flow(0, h).wait_recv()
-
-    @pl.when(has_prev)
-    def _():
-        stat_flow(1).wait_recv()
-
-        @pl.loop(0, HEADS)
-        def _(h):
-            result_flow(1, h).wait_recv()
-
-    below = jnp.zeros((HD - 16, 256), F32)
-    l_prev = jnp.transpose(jnp.concatenate([st_recv[0], below], axis=0))[:N]
-    l_next = jnp.transpose(jnp.concatenate([st_recv[1], below], axis=0))[:N]
-    l_own = st_parts[0, :N]
-    top = jnp.maximum(jnp.maximum(l_prev, l_next), l_own)
-    e_prev, e_next, e_own = jnp.exp(l_prev - top), jnp.exp(l_next - top), jnp.exp(l_own - top)
-    total = 1.0 / (e_prev + e_next + e_own)
-    e_prev, e_next, e_own = e_prev * total, e_next * total, e_own * total
-    for h in range(HEADS):
-        column = slice(h, h + 1)
-        att[:, h * HD : (h + 1) * HD] = (
-            e_own[:, column] * o_own[h]
-            + e_prev[:, column] * o_recv[0, h].astype(F32)
-            + e_next[:, column] * o_recv[1, h].astype(F32)
-        ).astype(BF16)
-
+        pl.when(h == EARLY - 1)(lambda: send_stats(0))
+
+    send_stats(1)
+
+    def collect(stage, first, last):
+        for which, has in ((0, has_next), (1, has_prev)):
+
+            @pl.when(has)
+            def _():
+                stat_flow(stage, which).wait_recv()
+
+                @pl.loop(first, last)
+                def _(h):
+                    result_flow(which, h).wait_recv()
+
+        below = jnp.zeros((HD - 16, 256), F32)
+        l_prev = jnp.transpose(jnp.concatenate([st_recv[stage, 0], below], axis=0))[:N]
+        l_next = jnp.transpose(jnp.concatenate([st_recv[stage, 1], below], axis=0))[:N]
+        l_own = st_parts[0, :N]
+        top = jnp.maximum(jnp.maximum(l_prev, l_next), l_own)
+        e_prev, e_next, e_own = jnp.exp2(l_prev - top), jnp.exp2(l_next - top), jnp.exp2(l_own - top)
+        total = 1.0 / (e_prev + e_next + e_own)
+        e_prev, e_next, e_own = e_prev * total, e_next * total, e_own * total
+        for h in range(first, last):
+            column = slice(h, h + 1)
+            att[:, h * HD : (h + 1) * HD] = (
+                e_own[:, column] * o_own[h]
+                + e_prev[:, column] * o_recv[0, h].astype(F32)
+                + e_next[:, column] * o_recv[1, h].astype(F32)
+            ).astype(BF16)
+
+    split = EARLY * HD
+    collect(0, 0, EARLY)
     for c in range(NCHUNK):
         weight_copy(3, c).wait()
+        acc = jnp.dot(att[:, :split], wo[c, :split], preferred_element_type=F32)
+        proj[2 * c] = acc[:, :HD]
+        proj[2 * c + 1] = acc[:, HD:]
+
+    collect(1, EARLY, HEADS)
+    for c in range(NCHUNK):
         columns = slice(c * CHUNK, (c + 1) * CHUNK)
+        early = jnp.concatenate([proj[2 * c], proj[2 * c + 1]], axis=1)
         out_ref[:, columns] = (
-            jnp.dot(att[...], wo[c], preferred_element_type=F32) * mod_ref[2:3, columns]
+            (early + jnp.dot(att[:, split:], wo[c, split:], preferred_element_type=F32)) * mod_ref[2:3, columns]
         ).astype(BF16)
 
     @pl.loop(0, HEADS)
@@ -398,13 +413,12 @@
             flow(own_ac, h).wait_send()
             flow(wd_ac, h).wait_send()
 
-        turn = turned(h)
-        straight = jnp.logical_not(turn)
-        pl.when(jnp.logical_and(has_to, straight))(lambda: flow(wd_to, h).wait_send())
-        pl.when(jnp.logical_and(inner_to, straight))(lambda: flow(ac_to, h).wait_send())
-        pl.when(jnp.logical_and(has_from, turn))(lambda: turn_flow(0, h).wait_send())
+        turn, ac_turn = turned(h), ac_turned(h)
+        pl.when(jnp.logical_and(has_to, jnp.logical_not(turn)))(lambda: flow(wd_to, h).wait_send())
+        pl.when(jnp.logical_and(inner_to, jnp.logical_not(ac_turn)))(lambda: flow(ac_to, h).wait_send())
+        pl.when(jnp.logical_and(has_from, in_transit(h)))(lambda: turn_flow(0, h).wait_send())
         pl.when(jnp.logical_and(has_to, turn))(lambda: turn_flow(1, h).wait_send())
-        pl.when(jnp.logical_and(inner_to, turn))(lambda: turn_flow(2, h).wait_send())
+        pl.when(jnp.logical_and(inner_to, ac_turn))(lambda: turn_flow(2, h).wait_send())
         pl.when(has_from)(lambda: flow(wz_sib, h).wait_send())
 
         @pl.when(has_next)
@@ -417,8 +431,9 @@
             query_flow(1, h).wait_send()
             result_flow(0, h).wait_send()
 
-    pl.when(has_prev)(lambda: stat_flow(0).wait_send())
-    pl.when(has_next)(lambda: stat_flow(1).wait_send())
+    for stage in range(2):
+        pl.when(has_prev)(lambda: stat_flow(stage, 0).wait_send())
+        pl.when(has_next)(lambda: stat_flow(stage, 1).wait_send())
 
 
 def body(tokens, modulation, w_query, w_key, w_value, w_out, norm_q, norm_k):
@@ -437,22 +452,22 @@
             pltpu.VMEM((HEADS, N, HD), F32),
             pltpu.VMEM((N, 3 * HD), F32),
             pltpu.VMEM((SLOTS, HEADS, N, 2 * HD), BF16),
-            pltpu.VMEM(((HEADS - TURN) // 2, N, 2 * HD), BF16),
+            pltpu.VMEM(((HEADS - AC_TURN) // 2, N, 2 * HD), BF16),
             pltpu.VMEM((SLOTS, N, HD), BF16),
             pltpu.VMEM((3, HEADS, N, HD), BF16),
             pltpu.VMEM((2, HEADS, N, HD), BF16),
             pltpu.VMEM((2, HEADS, N, HD), BF16),
             pltpu.VMEM((HEADS, N, HD), F32),
-            pltpu.VMEM((2, 16, 256), F32),
-            pltpu.VMEM((2, 16, 256), F32),
+            pltpu.VMEM((2, 2, 16, 256), F32),
+            pltpu.VMEM((2, 2, 16, 256), F32),
             pltpu.VMEM((3, 256, HD), F32),
             pltpu.VMEM((N, D), BF16),
             dma((4, NCHUNK)),
             dma((8, HEADS)), dma((8, HEADS)),
-            dma((3, (HEADS - TURN) // 2)), dma((3, (HEADS - TURN) // 2)),
+            dma((3, (HEADS - AC_TURN) // 2)), dma((3, (HEADS - AC_TURN) // 2)),
             dma((2, HEADS)), dma((2, HEADS)),
             dma((2, HEADS)), dma((2, HEADS)),
-            dma((2,)), dma((2,)),
+            dma((2, 2)), dma((2, 2)),
         ],
         compiler_params=pltpu.CompilerParams(
             collective_id=0, has_side_effects=True, vmem_limit_bytes=60 * 1024 * 1024

time: 69.6 us -> 66.5 us (0.955)
  Pallas kernels: 67.5 us -> 63.8 us
    pallas_call x1, Pallas kernels: 67.5 us -> 63.8 us  [body(): pl.pallas_call(kernel, out_shape=jax.ShapeDtypeStruct((N, D), BF16), in_s...]
where the time goes in v4:
time: 66.5 us; the launch traced here: 65.8 us
  Pallas kernels  63.8 us (96%)
  local copies, waits for them, and re-layouts  1.92 us (3%)
    pallas_call x1, Pallas kernels, body(): pl.pallas_call(kernel, out_shape=jax.ShapeDtypeStruct((N, D), BF16), in_s...  63.8 us
    unnamed x1, local copies, waits for them, and re-layouts  1.92 us

profile of v4, /device:TPU:90, one launch (start us, length us, event | category | flops | bytes accessed | tf_op | source)
XLA Modules:
  0.0 65.8 jit_solution(3470956782494389429)
XLA Ops:
  0.0 63.8 %tile_attention.1 = bf16[192,1536]{1,0:T(8,128)(2,1)} custom-call(bf16[192,1536]{1,0:T(8,128)(2,1)} %bitcast.3, f32[3,1536]{1,0:T(4,128)} %mod_ref.1, f32[1536]{0:T(1024)} %nq_ref.1, f32[1536]{0:T(1024)} %nk_ref.1, f32[16,8,384]{2,1,0:T(8,128)} %constant.2.clone.tab_ref, bf16[1536,1536]{1,0:T(8,128)(2,1)} %wq_hbm.1, bf16[1536,1536]{1,0:T(8,128)(2,1)} %wk_hbm.1, ...), custom_call_target="tpu_custom_call" | custom-call | tf_op jit(solution)/shard_map/tile_attention/pallas_call | solution.py:444
  63.8 1.9 %copy.11 = bf16[3,8,8,1536]{3,2,1,0:T(8,128)(2,1)} copy(bf16[3,8,8,1536]{3,2,1,0:T(8,128)(2,1)} %bitcast.2) | data formatting | bytes 1179648

commit v5 on v4

--- a/solution.py
+++ b/solution.py
@@ -220,12 +220,7 @@
         absent(WZ)
         absent(SIB_WZ)
 
-    @pl.when(jnp.logical_not(inner))
-    def _():
-        absent(AC_WD)
-        absent(AC)
-
-    @pl.when(jnp.logical_not(inner_from))
+    @pl.when(jnp.logical_and(inner, jnp.logical_not(has_from)))
     def _():
         absent(AC_WZ)
 
@@ -271,14 +266,6 @@
             device_id_type=MESH,
         )
 
-    inv_q = inverse(project(2, keep))
-
-    @pl.loop(0, HEADS)
-    def _(h):
-        q[0, h] = rotated(h, inv_q, nq_ref)
-        pl.when(has_next)(lambda: query_flow(0, h).start())
-        pl.when(has_prev)(lambda: query_flow(1, h).start())
-
     def pass_on(h):
         flow(own_wd, h).wait_recv()
         turn, ac_turn = turned(h), ac_turned(h)
@@ -304,7 +291,24 @@
             pl.when(turn)(lambda: turn_flow(1, h).wait_recv())
             flow(wz_sib, h).start()
 
-    for h in range(AHEAD):
+    inv_q = inverse(project(2, keep))
+    pass_on(0)
+
+    @pl.loop(0, HEADS // 2)
+    def _(h):
+        q[0, h] = rotated(h, inv_q, nq_ref)
+        pl.when(has_next)(lambda: query_flow(0, h).start())
+        pl.when(has_prev)(lambda: query_flow(1, h).start())
+
+    pass_on(1)
+
+    @pl.loop(HEADS // 2, HEADS)
+    def _(h):
+        q[0, h] = rotated(h, inv_q, nq_ref)
+        pl.when(has_next)(lambda: query_flow(0, h).start())
+        pl.when(has_prev)(lambda: query_flow(1, h).start())
+
+    for h in range(2, AHEAD):
         pass_on(h)
     for h in range(SHARE):
         share(h)
@@ -332,11 +336,11 @@
         pl.when(has_prev)(lambda: query_flow(0, h).wait_recv())
         pl.when(has_next)(lambda: query_flow(1, h).wait_recv())
 
-        keys = kv[:, h, :, :HD].reshape(SLOTS * N, HD)
-        values = jnp.concatenate(
-            [kv[:, h, :, HD:].reshape(SLOTS * N, HD), ones[...].reshape(SLOTS * N, HD)], axis=1
-        )
-        def attend(part):
+        def attend(part, slots):
+            keys = kv[:slots, h, :, :HD].reshape(slots * N, HD)
+            values = jnp.concatenate(
+                [kv[:slots, h, :, HD:].reshape(slots * N, HD), ones[:slots].reshape(slots * N, HD)], axis=1
+            )
             scores = lax.dot_general(
                 q[part, h], keys, (((1,), (1,)), ((), ())), preferred_element_type=F32
             )
@@ -347,13 +351,21 @@
             st_parts[part, :N] = jnp.where(lanes == h, stat, st_parts[part, :N])
             return acc[:, :HD] / acc[:, HD:]
 
-        for part in (1, 2):
-            o_send[part - 1, h] = attend(part).astype(BF16)
+        def other_frames(slots):
+            for part in (1, 2):
+                o_send[part - 1, h] = attend(part, slots).astype(BF16)
+
+        def own_frames(slots):
+            o_own[h] = attend(0, slots)
+
+        pl.when(inner)(lambda: other_frames(SLOTS))
+        pl.when(jnp.logical_not(inner))(lambda: other_frames(AC_WD))
         pl.when(has_prev)(lambda: result_flow(0, h).start())
         pl.when(has_next)(lambda: result_flow(1, h).start())
         pl.when(h + SHARE < HEADS)(lambda: share(h + SHARE))
         pl.when(jnp.logical_and(h % 2 == 1, ahead + 1 < HEADS))(lambda: pass_on(ahead + 1))
-        o_own[h] = attend(0)
+        pl.when(inner)(lambda: own_frames(SLOTS))
+        pl.when(jnp.logical_not(inner))(lambda: own_frames(AC_WD))
 
         pl.when(h == EARLY - 1)(lambda: send_stats(0))
 

time: 66.5 us -> 64.2 us (0.965)
  Pallas kernels: 63.8 us -> 62.1 us
    pallas_call x1, Pallas kernels: 63.8 us -> 62.1 us  [body(): pl.pallas_call(kernel, out_shape=jax.ShapeDtypeStruct((N, D), BF16), in_s...]
where the time goes in v5:
time: 64.2 us; the launch traced here: 64 us
  Pallas kernels  62.1 us (97%)
  local copies, waits for them, and re-layouts  1.92 us (3%)
    pallas_call x1, Pallas kernels, body(): pl.pallas_call(kernel, out_shape=jax.ShapeDtypeStruct((N, D), BF16), in_s...  62.1 us
    unnamed x1, local copies, waits for them, and re-layouts  1.92 us

profile of v5, /device:TPU:90, one launch (start us, length us, event | category | flops | bytes accessed | tf_op | source)
XLA Modules:
  0.0 64.0 jit_solution(4660410489086303510)
XLA Ops:
  0.0 62.1 %tile_attention.1 = bf16[192,1536]{1,0:T(8,128)(2,1)} custom-call(bf16[192,1536]{1,0:T(8,128)(2,1)} %bitcast.3, f32[3,1536]{1,0:T(4,128)} %mod_ref.1, f32[1536]{0:T(1024)} %nq_ref.1, f32[1536]{0:T(1024)} %nk_ref.1, f32[16,8,384]{2,1,0:T(8,128)} %constant.2.clone.tab_ref, bf16[1536,1536]{1,0:T(8,128)(2,1)} %wq_hbm.1, bf16[1536,1536]{1,0:T(8,128)(2,1)} %wk_hbm.1, ...), custom_call_target="tpu_custom_call" | custom-call | tf_op jit(solution)/shard_map/tile_attention/pallas_call | solution.py:456
  62.1 1.9 %copy.11 = bf16[3,8,8,1536]{3,2,1,0:T(8,128)(2,1)} copy(bf16[3,8,8,1536]{3,2,1,0:T(8,128)(2,1)} %bitcast.2) | data formatting | bytes 1179648

commit v6 on v5

--- a/solution.py
+++ b/solution.py
@@ -16,9 +16,9 @@
 OWN, WD, WZ, SIB, SIB_WD, SIB_WZ, AC_WD, AC, AC_WZ = range(SLOTS)
 AHEAD = 3
 SHARE = 1
-AT_ONCE = 4
+AT_ONCE = 6
 TURN = 8
-AC_TURN = 4
+AC_TURN = 0
 EARLY = 10
 MESH = pl.DeviceIdType.MESH
 F32 = jnp.float32

time: 64.2 us -> 61.3 us (0.955)
  Pallas kernels: 62.1 us -> 58.9 us
    pallas_call x1, Pallas kernels: 62.1 us -> 58.9 us  [body(): pl.pallas_call(kernel, out_shape=jax.ShapeDtypeStruct((N, D), BF16), in_s...]
where the time goes in v6:
time: 61.3 us; the launch traced here: 60.9 us
  Pallas kernels  58.9 us (96%)
  local copies, waits for them, and re-layouts  1.92 us (3%)
    pallas_call x1, Pallas kernels, body(): pl.pallas_call(kernel, out_shape=jax.ShapeDtypeStruct((N, D), BF16), in_s...  58.9 us
    unnamed x1, local copies, waits for them, and re-layouts  1.92 us

profile of v6, /device:TPU:90, one launch (start us, length us, event | category | flops | bytes accessed | tf_op | source)
XLA Modules:
  0.0 60.9 jit_solution(16605264112486368614)
XLA Ops:
  0.0 58.9 %tile_attention.1 = bf16[192,1536]{1,0:T(8,128)(2,1)} custom-call(bf16[192,1536]{1,0:T(8,128)(2,1)} %bitcast.3, f32[3,1536]{1,0:T(4,128)} %mod_ref.1, f32[1536]{0:T(1024)} %nq_ref.1, f32[1536]{0:T(1024)} %nk_ref.1, f32[16,8,384]{2,1,0:T(8,128)} %constant.2.clone.tab_ref, bf16[1536,1536]{1,0:T(8,128)(2,1)} %wq_hbm.1, bf16[1536,1536]{1,0:T(8,128)(2,1)} %wk_hbm.1, ...), custom_call_target="tpu_custom_call" | custom-call | tf_op jit(solution)/shard_map/tile_attention/pallas_call | solution.py:456
  58.9 1.9 %copy.11 = bf16[3,8,8,1536]{3,2,1,0:T(8,128)(2,1)} copy(bf16[3,8,8,1536]{3,2,1,0:T(8,128)(2,1)} %bitcast.2) | data formatting | bytes 1179648

commit v7 on v6

--- a/solution.py
+++ b/solution.py
@@ -16,7 +16,7 @@
 OWN, WD, WZ, SIB, SIB_WD, SIB_WZ, AC_WD, AC, AC_WZ = range(SLOTS)
 AHEAD = 3
 SHARE = 1
-AT_ONCE = 6
+AT_ONCE = 8
 TURN = 8
 AC_TURN = 0
 EARLY = 10

time: 61.3 us -> 63.4 us (1.034)
  the two profiles are of different devices: /device:TPU:90 before, /device:TPU:69 now
where the time goes in v7:
time: 63.4 us; the launch traced here: 63.3 us
  Pallas kernels  61.3 us (97%)
  local copies, waits for them, and re-layouts  1.92 us (3%)
    pallas_call x1, Pallas kernels, body(): pl.pallas_call(kernel, out_shape=jax.ShapeDtypeStruct((N, D), BF16), in_s...  61.3 us
    unnamed x1, local copies, waits for them, and re-layouts  1.92 us

profile of v7, /device:TPU:69, one launch (start us, length us, event | category | flops | bytes accessed | tf_op | source)
XLA Modules:
  0.0 63.3 jit_solution(10659040613355518727)
XLA Ops:
  0.0 61.3 %tile_attention.1 = bf16[192,1536]{1,0:T(8,128)(2,1)} custom-call(bf16[192,1536]{1,0:T(8,128)(2,1)} %bitcast.3, f32[3,1536]{1,0:T(4,128)} %mod_ref.1, f32[1536]{0:T(1024)} %nq_ref.1, f32[1536]{0:T(1024)} %nk_ref.1, f32[16,8,384]{2,1,0:T(8,128)} %constant.2.clone.tab_ref, bf16[1536,1536]{1,0:T(8,128)(2,1)} %wq_hbm.1, bf16[1536,1536]{1,0:T(8,128)(2,1)} %wk_hbm.1, ...), custom_call_target="tpu_custom_call" | custom-call | tf_op jit(solution)/shard_map/tile_attention/pallas_call | solution.py:456
  61.3 1.9 %copy.11 = bf16[3,8,8,1536]{3,2,1,0:T(8,128)(2,1)} copy(bf16[3,8,8,1536]{3,2,1,0:T(8,128)(2,1)} %bitcast.2) | data formatting | bytes 1179648
